TPU v7x, 256 devices: a whole 4x4x8 slice. The times are simulated.
256 devices in a mesh: ctx: 16 (over y, x), ch: 16 (over z, core).
Axes of the slice: x: 4, y: 4, z: 8, core: 2. Of those that a mesh axis runs over, the one named last changes fastest.
Arguments:
- qkv: bfloat16 [3, 512, 16384], P(None, 'ch', 'ctx'), may hold values from -6 to 6
- short_taps: float32 [3, 512, 7], P(None, 'ch'), may hold values from -2 to 2
- long_filter: float32 [512, 16384], P('ch', 'ctx'), may hold values from -0.046875 to 0.046875
- skip_gain: float32 [512], P('ch'), may hold values from -4 to 4
- out_weight: bfloat16 [8192, 512], P('ch'), may hold values from -0.25 to 0.25
Outputs:
- projected: bfloat16 [8192, 16384], P('ch', 'ctx')
All inputs are finite; a program needn't handle non-finite values.
Results may differ from a plain program's by a relative error of at most 0.0049.
Values may be sent and summed in bfloat16 or wider, within the bound.
A program may use at most 64 MiB of HBM per device.

v0:
```python
import functools

import jax
import jax.numpy as jnp
import ml_dtypes
import numpy as np
from jax import lax
from jax.experimental import pallas as pl
from jax.experimental.pallas import tpu as pltpu
from jax.sharding import PartitionSpec as P

MESH = pl.DeviceIdType.MESH
SIDE = 128
TAPS = 7
NODES = 16
ROUND = 8


def split(values):
    high = values.astype(ml_dtypes.bfloat16)
    low = (values - high.astype(np.float64)).astype(ml_dtypes.bfloat16)
    return high, low


def tables():
    k = np.arange(SIDE)[:, None]
    b = np.arange(SIDE)[None, :]
    total = SIDE * SIDE
    first = np.exp(2j * np.pi * (b / (4 * SIDE) - k * b / SIDE))
    twist = np.exp(2j * np.pi * (b / (4 * total) - k * b / total))
    middle = np.exp(-2j * np.pi * k * b / SIDE)
    last = np.conj(first).T / total
    first = np.concatenate([first.real, first.imag], 0)
    first = np.concatenate(split(first), 1)
    forward = np.block([[middle.real, middle.imag], [-middle.imag, middle.real]])
    inverse = np.block([[middle.real, -middle.imag], [middle.imag, middle.real]])
    last = np.concatenate([last.real, -last.imag], 1)
    return (
        first,
        np.stack([twist.real, twist.imag]).astype(np.float32),
        np.stack(split(forward)),
        np.stack(split(inverse)),
        np.stack(split(last)),
    )


def offsets():
    def far(step):
        return min(step, 4 - step)

    steps = [(dy, dx) for dy in range(4) for dx in range(4) if (dy, dx) != (0, 0)]
    return sorted(steps, key=lambda s: -(far(s[0]) + far(s[1])))


def parts(values):
    high = values.astype(jnp.bfloat16)
    return high, (values - high.astype(jnp.float32)).astype(jnp.bfloat16)


def mm(left, right):
    return jnp.dot(left, right, preferred_element_type=jnp.float32)


def kernel(
    qkv_in, taps_in, filt_in, skip_in, first_in, twist_in, fwd_in, inv_in, last_in,
    gath,
    qkv, taps, filt, skip, first, twist, fwd, inv, last,
    wide, send, recv, out_send, out_recv,
    load_sem, tab_sem, a_send, a_recv, q_send, q_recv, b_send, b_recv,
    up_send, up_recv, dn_send, dn_recv, pair_send, pair_recv,
):
    c = lax.axis_index("ctx")
    h = lax.axis_index("ch")
    y, x = c // 4, c % 4
    core = h % 2
    z = h // 2
    partner = h + 1 - 2 * core
    above = ((z + 1) % ROUND) * 2 + core
    below = ((z + ROUND - 1) % ROUND) * 2 + core
    steps = offsets()
    targets = [((y + dy) % 4) * 4 + (x + dx) % 4 for dy, dx in steps]
    sources = [((y + 4 - dy) % 4) * 4 + (x + 4 - dx) % 4 for dy, dx in steps]

    loads = [
        pltpu.make_async_copy(src, dst, load_sem.at[i])
        for i, (src, dst) in enumerate([(qkv_in, qkv), (filt_in, filt)])
    ]
    pairs = [(taps_in, taps), (skip_in, skip), (first_in, first), (twist_in, twist),
             (fwd_in, fwd), (inv_in, inv), (last_in, last)]
    others = [
        pltpu.make_async_copy(src, dst, tab_sem.at[i])
        for i, (src, dst) in enumerate(pairs)
    ]
    for copy in loads:
        copy.start()

    barrier = pltpu.get_barrier_semaphore()
    for target in targets:
        pl.semaphore_signal(barrier, inc=1, device_id={"ctx": target}, device_id_type=MESH)
    for target in (above, below, partner):
        pl.semaphore_signal(barrier, inc=1, device_id={"ch": target}, device_id_type=MESH)
    for copy in others:
        copy.start()
    for copy in loads:
        copy.wait()

    for stream in (1, 2, 3, 0):
        for row in range(8):
            lanes = slice(row * SIDE, (row + 1) * SIDE)
            block = filt[:, lanes] if stream == 3 else qkv[stream, :, lanes]
            wide[pl.ds(row, 32, stride=8), :] = block.astype(jnp.float32)
        send[:, stream] = wide[...].reshape(NODES, 16, SIDE).astype(jnp.bfloat16)

    pl.semaphore_wait(barrier, NODES - 1 + 3)
    a_copies = [
        pltpu.make_async_remote_copy(
            src_ref=send.at[target, 1:4],
            dst_ref=recv.at[c, 1:4],
            send_sem=a_send.at[i],
            recv_sem=a_recv.at[i],
            device_id={"ctx": target},
            device_id_type=MESH,
        )
        for i, target in enumerate(targets)
    ]
    q_copies = [
        pltpu.make_async_remote_copy(
            src_ref=send.at[target, 0:1],
            dst_ref=recv.at[c, 0:1],
            send_sem=q_send.at[i],
            recv_sem=q_recv.at[i],
            device_id={"ctx": target},
            device_id_type=MESH,
        )
        for i, target in enumerate(targets)
    ]
    for copy in a_copies:
        copy.start()
    for copy in q_copies:
        copy.start()
    recv[c] = send[c]
    for copy in others:
        copy.wait()

    lane = lax.broadcasted_iota(jnp.int32, (SIDE, SIDE), 1)
    line = lax.broadcasted_iota(jnp.int32, (SIDE, SIDE), 0)

    def stream_of(stream):
        both = recv[:, stream].astype(jnp.float32).reshape(NODES, 2, 8, SIDE)
        return [both[:, n].reshape(SIDE, SIDE) for n in range(2)]

    def short(values, stream, n):
        before = jnp.where(line == 0, 0.0, pltpu.roll(values, 1, 0))
        tap = taps[stream, pl.ds(2 * c + n, 1), :]
        total = tap[:, 0:1] * values
        for j in range(1, TAPS):
            mixed = jnp.where(lane >= SIDE - j, before, values)
            total = total + tap[:, j : j + 1] * pltpu.roll(mixed, j, 1)
        return total

    twist_re, twist_im = twist[0], twist[1]

    def turned(real, imag):
        return jnp.concatenate(
            [real * twist_re - imag * twist_im, real * twist_im + imag * twist_re], axis=1
        )

    def spectrum(signals):
        data = jnp.concatenate(signals, axis=1)
        head = mm(first[...], jnp.concatenate([data, data], axis=0))
        rows = [
            turned(head[:SIDE, i * SIDE : (i + 1) * SIDE], head[SIDE:, i * SIDE : (i + 1) * SIDE])
            for i in range(len(signals))
        ]
        high, low = parts(jnp.concatenate(rows, axis=0))
        return mm(high, fwd[0]) + mm(low, fwd[0]) + mm(high, fwd[1])

    for copy in a_copies:
        copy.wait_recv()
    filter_rows = recv[:, 3].reshape(NODES, 2, 8, SIDE)
    filters = [filter_rows[:, n].reshape(SIDE, SIDE) for n in range(2)]
    spec_f = spectrum(filters)
    k_rows, v_rows = stream_of(1), stream_of(2)
    product = [short(k_rows[n], 1, n) * short(v_rows[n], 2, n) for n in range(2)]
    spec_p = spectrum([p.astype(jnp.bfloat16) for p in product])
    p_re, p_im = spec_p[:, :SIDE], spec_p[:, SIDE:]
    f_re, f_im = spec_f[:, :SIDE], spec_f[:, SIDE:]
    joined = jnp.concatenate([p_re * f_re - p_im * f_im, p_re * f_im + p_im * f_re], axis=1)
    high, low = parts(joined)
    back = mm(high, inv[0]) + mm(low, inv[0]) + mm(high, inv[1])
    columns = []
    for n in range(2):
        real = back[n * SIDE : (n + 1) * SIDE, :SIDE]
        imag = back[n * SIDE : (n + 1) * SIDE, SIDE:]
        columns.append(
            jnp.concatenate(
                [real * twist_re + imag * twist_im, imag * twist_re - real * twist_im], axis=0
            )
        )
    high, low = parts(jnp.concatenate(columns, axis=1))
    convolved = mm(last[0], high) + mm(last[1], high) + mm(last[0], low)

    for copy in q_copies:
        copy.wait_recv()
    q_rows = stream_of(0)
    gated = []
    for n in range(2):
        query = short(q_rows[n], 0, n)
        mixed = convolved[:, n * SIDE : (n + 1) * SIDE] + skip[2 * c + n] * product[n]
        gated.append((query * mixed).reshape(NODES, 1, 8, SIDE))
    out_send[...] = (
        jnp.concatenate(gated, axis=1).reshape(NODES, 16, SIDE).astype(jnp.bfloat16)
    )

    b_copies = [
        pltpu.make_async_remote_copy(
            src_ref=out_send.at[target],
            dst_ref=out_recv.at[c],
            send_sem=b_send.at[i],
            recv_sem=b_recv.at[i],
            device_id={"ctx": target},
            device_id_type=MESH,
        )
        for i, target in enumerate(targets)
    ]
    for copy in b_copies:
        copy.start()
    out_recv[c] = out_send[c]
    for copy in b_copies:
        copy.wait_recv()

    wide[...] = out_recv[...].astype(jnp.float32).reshape(2 * SIDE, SIDE)
    for row in range(8):
        gath[h, :, row * SIDE : (row + 1) * SIDE] = wide[pl.ds(row, 32, stride=8), :].astype(
            jnp.bfloat16
        )

    def ring(owner, half, send_sem, recv_sem, index, target):
        block = gath.at[owner, pl.ds(half * 16, 16)]
        return pltpu.make_async_remote_copy(
            src_ref=block,
            dst_ref=block,
            send_sem=send_sem.at[index, half],
            recv_sem=recv_sem.at[index, half],
            device_id={"ch": target},
            device_id_type=MESH,
        )

    up_steps, dn_steps = (4, 3), (3, 4)
    started = []
    pair_index = {}

    def to_partner(index, half, owner):
        copy = ring(owner, half, pair_send, pair_recv, index, partner)
        copy.start()
        started.append(copy)

    for half in range(2):
        for copy in (
            ring(h, half, up_send, up_recv, 0, above),
            ring(h, half, dn_send, dn_recv, 0, below),
        ):
            copy.start()
            started.append(copy)
        to_partner(0, half, h)
    for step in range(1, 5):
        for half in range(2):
            for limit, s_sem, r_sem, target, sign in (
                (up_steps[half], up_send, up_recv, above, -1),
                (dn_steps[half], dn_send, dn_recv, below, 1),
            ):
                if step > limit:
                    continue
                owner = ((z + ROUND + sign * step) % ROUND) * 2 + core
                ring(owner, half, s_sem, r_sem, step - 1, target).wait_recv()
                if step < limit:
                    copy = ring(owner, half, s_sem, r_sem, step, target)
                    copy.start()
                    started.append(copy)
                to_partner(step if sign < 0 else 4 + step, half, owner)
    for half in range(2):
        ring(h, half, pair_send, pair_recv, 0, partner).wait_recv()
    for step in range(1, 5):
        for half in range(2):
            for limit, sign in ((up_steps[half], -1), (dn_steps[half], 1)):
                if step > limit:
                    continue
                index = step if sign < 0 else 4 + step
                ring(h, half, pair_send, pair_recv, index, partner).wait_recv()
    for copy in a_copies + q_copies + b_copies + started:
        copy.wait_send()


def solution(mesh):
    consts = tables()
    dma = pltpu.SemaphoreType.DMA
    peers = NODES - 1

    def local(qkv, short_taps, long_filter, skip_gain, out_weight):
        gathered = pl.pallas_call(
            kernel,
            out_shape=jax.ShapeDtypeStruct((NODES, 32, 1024), jnp.bfloat16),
            in_specs=[pl.BlockSpec(memory_space=pl.ANY)] * 9,
            out_specs=pl.BlockSpec(memory_space=pltpu.VMEM),
            scratch_shapes=[
                pltpu.VMEM((3, 32, 1024), jnp.bfloat16),
                pltpu.VMEM((3, 32, TAPS), jnp.float32),
                pltpu.VMEM((32, 1024), jnp.float32),
                pltpu.SMEM((32,), jnp.float32),
                pltpu.VMEM((256, 256), jnp.bfloat16),
                pltpu.VMEM((2, SIDE, SIDE), jnp.float32),
                pltpu.VMEM((2, 256, 256), jnp.bfloat16),
                pltpu.VMEM((2, 256, 256), jnp.bfloat16),
                pltpu.VMEM((2, SIDE, 256), jnp.bfloat16),
                pltpu.VMEM((256, SIDE), jnp.float32),
                pltpu.VMEM((NODES, 4, 16, SIDE), jnp.bfloat16),
                pltpu.VMEM((NODES, 4, 16, SIDE), jnp.bfloat16),
                pltpu.VMEM((NODES, 16, SIDE), jnp.bfloat16),
                pltpu.VMEM((NODES, 16, SIDE), jnp.bfloat16),
                dma((2,)),
                dma((7,)),
                dma((peers,)),
                dma((peers,)),
                dma((peers,)),
                dma((peers,)),
                dma((peers,)),
                dma((peers,)),
                dma((4, 2)),
                dma((4, 2)),
                dma((4, 2)),
                dma((4, 2)),
                dma((9, 2)),
                dma((9, 2)),
            ],
            compiler_params=pltpu.CompilerParams(collective_id=0, has_side_effects=True),
        )(qkv, short_taps, long_filter, skip_gain, *[jnp.asarray(t) for t in consts])
        summed = jnp.dot(
            out_weight,
            gathered.reshape(NODES * 32, 1024),
            preferred_element_type=jnp.float32,
        )
        return summed.astype(jnp.bfloat16)

    placed = (P(None, "ch", "ctx"), P(None, "ch", None), P("ch", "ctx"), P("ch"), P("ch", None))
    return jax.shard_map(
        local, mesh=mesh, in_specs=placed, out_specs=P("ch", "ctx"), check_vma=False
    )
```

profile of v0, /device:TPU:1, one launch (start us, length us, event | category | flops | bytes accessed | tf_op | source)
XLA Modules:
  0.0 43.9 jit_solution(12159177145339550350)
XLA Ops:
  0.0 0.0 copy-start
  0.0 1.5 %copy.11.taps_in = f32[3,32,7]{2,1,0:T(8,128)} copy(f32[3,32,7]{1,2,0:T(8,128)} %param.11) | data formatting | bytes 5376 | tf_op args[1]
  1.5 39.1 %shard_map.100 = bf16[16,32,1024]{2,1,0:T(8,128)(2,1)} custom-call(bf16[3,32,1024]{2,1,0:T(8,128)(2,1)} %qkv_in.1, f32[3,32,7]{2,1,0:T(8,128)} %copy.11.taps_in, f32[32,1024]{1,0:T(8,128)} %filt_in.1, f32[32]{0:T(128)} %skip_in.1, bf16[256,256]{1,0:T(8,128)(2,1)} %constant.10.clone.first_in, f32[2,128,128]{2,1,0:T(8,128)} %constant.11.clone.twist_in, ...), custom_call_target="tpu_custom_call" | custom-call | tf_op jit(solution)/shard_map/pallas_call | solution.py:300
  40.6 0.0 copy-done
  40.6 2.0 %fusion = bf16[512,1024]{0,1:T(8,128)(2,1)S(1)} fusion(bf16[512,1024]{1,0:T(8,128)(2,1)} %bitcast.5, bf16[512,512]{1,0:T(8,128)(2,1)S(1)} %copy-done), kind=kOutput, calls=%fused_computation.1 | convolution fusion | flops 537395200 | bytes 2621440 | tf_op jit(solution)/shard_map/dot_general | solution.py:337
  42.6 1.3 %copy.12 = bf16[512,1024]{1,0:T(8,128)(2,1)} copy(bf16[512,1024]{0,1:T(8,128)(2,1)S(1)} %fusion) | data formatting | bytes 2097152 | tf_op jit(solution)/shard_map/convert_element_type | solution.py:342
Async XLA Ops:
  0.0 40.6 %copy-start = (bf16[512,512]{1,0:T(8,128)(2,1)S(1)}, bf16[512,512]{1,0:T(8,128)(2,1)}, u32[]{:S(2)}) copy-start(bf16[512,512]{1,0:T(8,128)(2,1)} %param.14) | copy-start | bytes 1572868
where the time goes:
time: 44 us; the launch traced here: 43.9 us
  Pallas kernels  39.1 us (89%)
  local copies, waits for them, and re-layouts  2.8 us (6%)
  matrix products  1.98 us (4%)
    pallas_call x1, Pallas kernels, local(): pl.pallas_call(kernel, out_shape=jax.ShapeDtypeStruct((NODES, 32, 1024),...  39.1 us
    dot_general x1, matrix products, local(): jnp.dot(out_weight, gathered.reshape(NODES * 32, 1024), preferred_element...  1.98 us
    unnamed x3, local copies, waits for them, and re-layouts  1.48 us
    convert_element_type x1, local copies, waits for them, and re-layouts, local(): return summed.astype(jnp.bfloat16)  1.32 us

commit v1 on v0

--- a/solution.py
+++ b/solution.py
@@ -67,7 +67,7 @@
     qkv, taps, filt, skip, first, twist, fwd, inv, last,
     wide, send, recv, out_send, out_recv,
     load_sem, tab_sem, a_send, a_recv, q_send, q_recv, b_send, b_recv,
-    up_send, up_recv, dn_send, dn_recv, pair_send, pair_recv,
+    z_send, z_recv, pair_send, pair_recv,
 ):
     c = lax.axis_index("ctx")
     h = lax.axis_index("ch")
@@ -75,12 +75,14 @@
     core = h % 2
     z = h // 2
     partner = h + 1 - 2 * core
-    above = ((z + 1) % ROUND) * 2 + core
-    below = ((z + ROUND - 1) % ROUND) * 2 + core
+    def plane(jump):
+        return ((z + ROUND + jump) % ROUND) * 2 + core
+
     steps = offsets()
     targets = [((y + dy) % 4) * 4 + (x + dx) % 4 for dy, dx in steps]
     sources = [((y + 4 - dy) % 4) * 4 + (x + 4 - dx) % 4 for dy, dx in steps]
 
+    sent = []
     loads = [
         pltpu.make_async_copy(src, dst, load_sem.at[i])
         for i, (src, dst) in enumerate([(qkv_in, qkv), (filt_in, filt)])
@@ -97,8 +99,17 @@
     barrier = pltpu.get_barrier_semaphore()
     for target in targets:
         pl.semaphore_signal(barrier, inc=1, device_id={"ctx": target}, device_id_type=MESH)
-    for target in (above, below, partner):
-        pl.semaphore_signal(barrier, inc=1, device_id={"ch": target}, device_id_type=MESH)
+    for jump in (1, -1, 2, -2):
+        pl.semaphore_signal(barrier, inc=1, device_id={"ch": plane(jump)}, device_id_type=MESH)
+    pl.semaphore_signal(barrier, inc=1, device_id={"ch": partner}, device_id_type=MESH)
+    for jump in (2, -2):
+        for target in targets:
+            pl.semaphore_signal(
+                barrier,
+                inc=1,
+                device_id={"ctx": target, "ch": plane(jump)},
+                device_id_type=MESH,
+            )
     for copy in others:
         copy.start()
     for copy in loads:
@@ -111,7 +122,7 @@
             wide[pl.ds(row, 32, stride=8), :] = block.astype(jnp.float32)
         send[:, stream] = wide[...].reshape(NODES, 16, SIDE).astype(jnp.bfloat16)
 
-    pl.semaphore_wait(barrier, NODES - 1 + 3)
+    pl.semaphore_wait(barrier, 3 * (NODES - 1) + 5)
     a_copies = [
         pltpu.make_async_remote_copy(
             src_ref=send.at[target, 1:4],
@@ -138,11 +149,13 @@
         copy.start()
     for copy in q_copies:
         copy.start()
+    sent += a_copies + q_copies
     recv[c] = send[c]
     for copy in others:
         copy.wait()
 
     lane = lax.broadcasted_iota(jnp.int32, (SIDE, SIDE), 1)
+    spot = lax.broadcasted_iota(jnp.int32, (TAPS, 32), 1)
     line = lax.broadcasted_iota(jnp.int32, (SIDE, SIDE), 0)
 
     def stream_of(stream):
@@ -151,11 +164,11 @@
 
     def short(values, stream, n):
         before = jnp.where(line == 0, 0.0, pltpu.roll(values, 1, 0))
-        tap = taps[stream, pl.ds(2 * c + n, 1), :]
-        total = tap[:, 0:1] * values
+        tap = jnp.sum(jnp.where(spot == 2 * c + n, taps[stream], 0.0), axis=1, keepdims=True)
+        total = tap[0:1] * values
         for j in range(1, TAPS):
             mixed = jnp.where(lane >= SIDE - j, before, values)
-            total = total + tap[:, j : j + 1] * pltpu.roll(mixed, j, 1)
+            total = total + tap[j : j + 1] * pltpu.roll(mixed, j, 1)
         return total
 
     twist_re, twist_im = twist[0], twist[1]
@@ -212,83 +225,78 @@
         jnp.concatenate(gated, axis=1).reshape(NODES, 16, SIDE).astype(jnp.bfloat16)
     )
 
-    b_copies = [
-        pltpu.make_async_remote_copy(
-            src_ref=out_send.at[target],
-            dst_ref=out_recv.at[c],
-            send_sem=b_send.at[i],
-            recv_sem=b_recv.at[i],
-            device_id={"ctx": target},
-            device_id_type=MESH,
-        )
-        for i, target in enumerate(targets)
-    ]
-    for copy in b_copies:
-        copy.start()
-    out_recv[c] = out_send[c]
-    for copy in b_copies:
-        copy.wait_recv()
-
-    wide[...] = out_recv[...].astype(jnp.float32).reshape(2 * SIDE, SIDE)
-    for row in range(8):
-        gath[h, :, row * SIDE : (row + 1) * SIDE] = wide[pl.ds(row, 32, stride=8), :].astype(
-            jnp.bfloat16
-        )
-
-    def ring(owner, half, send_sem, recv_sem, index, target):
-        block = gath.at[owner, pl.ds(half * 16, 16)]
+    jumps = (0, 2, -2)
+    b_copies = []
+    for group, jump in enumerate(jumps):
+        copies = [
+            pltpu.make_async_remote_copy(
+                src_ref=out_send.at[target],
+                dst_ref=out_recv.at[group, c],
+                send_sem=b_send.at[group, i],
+                recv_sem=b_recv.at[group, i],
+                device_id={"ctx": target, "ch": plane(jump)},
+                device_id_type=MESH,
+            )
+            for i, target in enumerate(targets + ([c] if jump else []))
+        ]
+        b_copies.append(copies)
+    for group in (1, 2, 0):
+        for copy in b_copies[group]:
+            copy.start()
+        sent += b_copies[group]
+    out_recv[0, c] = out_send[c]
+
+    def hop(owner, part, send_sem, recv_sem, index, target):
+        block = gath.at[owner] if part is None else gath.at[owner, pl.ds(part * 16, 16)]
         return pltpu.make_async_remote_copy(
             src_ref=block,
             dst_ref=block,
-            send_sem=send_sem.at[index, half],
-            recv_sem=recv_sem.at[index, half],
+            send_sem=send_sem.at[index],
+            recv_sem=recv_sem.at[index],
             device_id={"ch": target},
             device_id_type=MESH,
         )
 
-    up_steps, dn_steps = (4, 3), (3, 4)
-    started = []
-    pair_index = {}
-
-    def to_partner(index, half, owner):
-        copy = ring(owner, half, pair_send, pair_recv, index, partner)
-        copy.start()
-        started.append(copy)
-
-    for half in range(2):
-        for copy in (
-            ring(h, half, up_send, up_recv, 0, above),
-            ring(h, half, dn_send, dn_recv, 0, below),
-        ):
-            copy.start()
-            started.append(copy)
-        to_partner(0, half, h)
-    for step in range(1, 5):
-        for half in range(2):
-            for limit, s_sem, r_sem, target, sign in (
-                (up_steps[half], up_send, up_recv, above, -1),
-                (dn_steps[half], dn_send, dn_recv, below, 1),
-            ):
-                if step > limit:
-                    continue
-                owner = ((z + ROUND + sign * step) % ROUND) * 2 + core
-                ring(owner, half, s_sem, r_sem, step - 1, target).wait_recv()
-                if step < limit:
-                    copy = ring(owner, half, s_sem, r_sem, step, target)
-                    copy.start()
-                    started.append(copy)
-                to_partner(step if sign < 0 else 4 + step, half, owner)
-    for half in range(2):
-        ring(h, half, pair_send, pair_recv, 0, partner).wait_recv()
-    for step in range(1, 5):
-        for half in range(2):
-            for limit, sign in ((up_steps[half], -1), (dn_steps[half], 1)):
-                if step > limit:
-                    continue
-                index = step if sign < 0 else 4 + step
-                ring(h, half, pair_send, pair_recv, index, partner).wait_recv()
-    for copy in a_copies + q_copies + b_copies + started:
+    def begin(copy):
+        copy.start()
+        sent.append(copy)
+
+    def share(index, owner, part=None):
+        begin(hop(owner, part, pair_send, pair_recv, index, partner))
+
+    for group, jump in enumerate(jumps):
+        for copy in b_copies[group]:
+            copy.wait_recv()
+        owner = plane(-jump)
+        wide[...] = out_recv[group].astype(jnp.float32).reshape(2 * SIDE, SIDE)
+        for row in range(8):
+            gath[owner, :, row * SIDE : (row + 1) * SIDE] = wide[
+                pl.ds(row, 32, stride=8), :
+            ].astype(jnp.bfloat16)
+        if jump == 0:
+            begin(hop(owner, None, z_send, z_recv, 0, plane(1)))
+            begin(hop(owner, None, z_send, z_recv, 1, plane(-1)))
+        elif jump > 0:
+            begin(hop(owner, 0, z_send, z_recv, 4, plane(2)))
+            begin(hop(owner, None, z_send, z_recv, 2, plane(1)))
+        else:
+            begin(hop(owner, 1, z_send, z_recv, 5, plane(-2)))
+            begin(hop(owner, None, z_send, z_recv, 3, plane(-1)))
+        share(group, owner)
+    for index, jump, part in (
+        (0, -1, None), (1, 1, None), (2, -3, None), (3, 3, None), (4, 4, 0), (5, 4, 1),
+    ):
+        owner = plane(jump)
+        hop(owner, part, z_send, z_recv, index, plane(1)).wait_recv()
+        share(3 + index, owner, part)
+    for index, part in enumerate((None,) * 7 + (0, 1)):
+        hop(h, part, pair_send, pair_recv, index, partner).wait_recv()
+    for copy in sent:
         copy.wait_send()
+
+
+def project(weight, values, out):
+    out[...] = mm(weight[...], values[...]).astype(jnp.bfloat16)
 
 
 def solution(mesh):
@@ -304,7 +312,7 @@
             out_specs=pl.BlockSpec(memory_space=pltpu.VMEM),
             scratch_shapes=[
                 pltpu.VMEM((3, 32, 1024), jnp.bfloat16),
-                pltpu.VMEM((3, 32, TAPS), jnp.float32),
+                pltpu.VMEM((3, TAPS, 32), jnp.float32),
                 pltpu.VMEM((32, 1024), jnp.float32),
                 pltpu.SMEM((32,), jnp.float32),
                 pltpu.VMEM((256, 256), jnp.bfloat16),
@@ -316,30 +324,32 @@
                 pltpu.VMEM((NODES, 4, 16, SIDE), jnp.bfloat16),
                 pltpu.VMEM((NODES, 4, 16, SIDE), jnp.bfloat16),
                 pltpu.VMEM((NODES, 16, SIDE), jnp.bfloat16),
-                pltpu.VMEM((NODES, 16, SIDE), jnp.bfloat16),
+                pltpu.VMEM((3, NODES, 16, SIDE), jnp.bfloat16),
                 dma((2,)),
                 dma((7,)),
                 dma((peers,)),
                 dma((peers,)),
                 dma((peers,)),
                 dma((peers,)),
-                dma((peers,)),
-                dma((peers,)),
-                dma((4, 2)),
-                dma((4, 2)),
-                dma((4, 2)),
-                dma((4, 2)),
-                dma((9, 2)),
-                dma((9, 2)),
+                dma((3, NODES)),
+                dma((3, NODES)),
+                dma((6,)),
+                dma((6,)),
+                dma((9,)),
+                dma((9,)),
             ],
             compiler_params=pltpu.CompilerParams(collective_id=0, has_side_effects=True),
-        )(qkv, short_taps, long_filter, skip_gain, *[jnp.asarray(t) for t in consts])
-        summed = jnp.dot(
-            out_weight,
-            gathered.reshape(NODES * 32, 1024),
-            preferred_element_type=jnp.float32,
-        )
-        return summed.astype(jnp.bfloat16)
+        )(qkv, jnp.swapaxes(short_taps, 1, 2), long_filter, skip_gain, *[jnp.asarray(t) for t in consts])
+        return pl.pallas_call(
+            project,
+            grid=(4,),
+            out_shape=jax.ShapeDtypeStruct((512, 1024), jnp.bfloat16),
+            in_specs=[
+                pl.BlockSpec((512, 512), lambda i: (0, 0)),
+                pl.BlockSpec((512, 256), lambda i: (0, i)),
+            ],
+            out_specs=pl.BlockSpec((512, 256), lambda i: (0, i)),
+        )(out_weight, gathered.reshape(NODES * 32, 1024))
 
     placed = (P(None, "ch", "ctx"), P(None, "ch", None), P("ch", "ctx"), P("ch"), P("ch", None))
     return jax.shard_map(

time: 44 us -> 37.8 us (0.86)
  local copies, waits for them, and re-layouts: 2.8 us -> 0 us
  matrix products: 1.98 us -> 0 us
  Pallas kernels: 39.1 us -> 37.6 us
    pallas_call x1, Pallas kernels: 39.1 us -> 33.5 us  [local(): pl.pallas_call(kernel, out_shape=jax.ShapeDtypeStruct((NODES, 32, 1024),...]
    pallas_call x0 -> x1, Pallas kernels: none -> 4.11 us  [local(): pl.pallas_call(project, grid=(4,), out_shape=jax.ShapeDtypeStruct((512, 1...]
    dot_general x1 -> x0, matrix products: 1.98 us -> none  [local(): jnp.dot(out_weight, gathered.reshape(NODES * 32, 1024), preferred_element...]
    unnamed x3 -> x0, local copies, waits for them, and re-layouts: 1.48 us -> none
    convert_element_type x1 -> x0, local copies, waits for them, and re-layouts: 1.32 us -> none  [local(): return summed.astype(jnp.bfloat16)]
where the time goes in v1:
time: 37.8 us; the launch traced here: 37.6 us
  Pallas kernels  37.6 us (99%)
    pallas_call x1, Pallas kernels, local(): pl.pallas_call(kernel, out_shape=jax.ShapeDtypeStruct((NODES, 32, 1024),...  33.5 us
    pallas_call x1, Pallas kernels, local(): pl.pallas_call(project, grid=(4,), out_shape=jax.ShapeDtypeStruct((512, 1...  4.11 us

profile of v1, /device:TPU:1, one launch (start us, length us, event | category | flops | bytes accessed | tf_op | source)
XLA Modules:
  0.0 37.6 jit_solution(7207376607430237347)
XLA Ops:
  0.0 33.5 %shard_map.100 = bf16[16,32,1024]{2,1,0:T(8,128)(2,1)} custom-call(bf16[3,32,1024]{2,1,0:T(8,128)(2,1)} %qkv_in.1, f32[3,7,32]{2,1,0:T(8,128)} %bitcast.3, f32[32,1024]{1,0:T(8,128)} %filt_in.1, f32[32]{0:T(128)} %skip_in.1, bf16[256,256]{1,0:T(8,128)(2,1)} %constant.10.clone.first_in, f32[2,128,128]{2,1,0:T(8,128)} %constant.11.clone.twist_in, ...), custom_call_target="tpu_custom_call" | custom-call | tf_op jit(solution)/shard_map/pallas_call | solution.py:308
  33.5 4.1 %shard_map.101 = bf16[512,1024]{1,0:T(8,128)(2,1)} custom-call(bf16[512,512]{1,0:T(8,128)(2,1)} %weight.1, bf16[512,1024]{1,0:T(8,128)(2,1)} %bitcast.2), custom_call_target="tpu_custom_call" | custom-call | tf_op jit(solution)/shard_map/pallas_call | solution.py:343

commit v2 on v1

--- a/solution.py
+++ b/solution.py
@@ -14,6 +14,8 @@
 TAPS = 7
 NODES = 16
 ROUND = 8
+GRANT = 16 << 20
+CHUNK = 256
 
 
 def split(values):
@@ -62,12 +64,12 @@
 
 
 def kernel(
-    qkv_in, taps_in, filt_in, skip_in, first_in, twist_in, fwd_in, inv_in, last_in,
-    gath,
+    qkv_in, taps_in, filt_in, skip_in, weight_in, first_in, twist_in, fwd_in, inv_in, last_in,
+    out,
     qkv, taps, filt, skip, first, twist, fwd, inv, last,
-    wide, send, recv, out_send, out_recv,
+    weight, picked, gath, total, wide, send, recv, out_send, out_recv,
     load_sem, tab_sem, a_send, a_recv, q_send, q_recv, b_send, b_recv,
-    z_send, z_recv, pair_send, pair_recv,
+    z_send, z_recv, pair_send, pair_recv, ready,
 ):
     c = lax.axis_index("ctx")
     h = lax.axis_index("ch")
@@ -88,7 +90,7 @@
         for i, (src, dst) in enumerate([(qkv_in, qkv), (filt_in, filt)])
     ]
     pairs = [(taps_in, taps), (skip_in, skip), (first_in, first), (twist_in, twist),
-             (fwd_in, fwd), (inv_in, inv), (last_in, last)]
+             (fwd_in, fwd), (inv_in, inv), (last_in, last), (weight_in, weight)]
     others = [
         pltpu.make_async_copy(src, dst, tab_sem.at[i])
         for i, (src, dst) in enumerate(pairs)
@@ -102,14 +104,6 @@
     for jump in (1, -1, 2, -2):
         pl.semaphore_signal(barrier, inc=1, device_id={"ch": plane(jump)}, device_id_type=MESH)
     pl.semaphore_signal(barrier, inc=1, device_id={"ch": partner}, device_id_type=MESH)
-    for jump in (2, -2):
-        for target in targets:
-            pl.semaphore_signal(
-                barrier,
-                inc=1,
-                device_id={"ctx": target, "ch": plane(jump)},
-                device_id_type=MESH,
-            )
     for copy in others:
         copy.start()
     for copy in loads:
@@ -122,7 +116,9 @@
             wide[pl.ds(row, 32, stride=8), :] = block.astype(jnp.float32)
         send[:, stream] = wide[...].reshape(NODES, 16, SIDE).astype(jnp.bfloat16)
 
-    pl.semaphore_wait(barrier, 3 * (NODES - 1) + 5)
+    pl.semaphore_wait(barrier, NODES - 1 + 5)
+    for jump in (1, -1, 2, -2):
+        pl.semaphore_signal(ready, inc=1, device_id={"ch": plane(jump)}, device_id_type=MESH)
     a_copies = [
         pltpu.make_async_remote_copy(
             src_ref=send.at[target, 1:4],
@@ -153,6 +149,13 @@
     recv[c] = send[c]
     for copy in others:
         copy.wait()
+
+    wanted = lax.broadcasted_iota(jnp.int32, (512, 512), 1)
+    holder = (wanted // 256 + core) % 2
+    wanted = (wanted // 32) % ROUND * 64 + holder * 32 + wanted % 32
+    given = lax.broadcasted_iota(jnp.int32, (512, 512), 0)
+    chosen = jnp.where(given == wanted, 1.0, 0.0).astype(jnp.bfloat16)
+    picked[...] = mm(weight[...], chosen).astype(jnp.bfloat16)
 
     lane = lax.broadcasted_iota(jnp.int32, (SIDE, SIDE), 1)
     spot = lax.broadcasted_iota(jnp.int32, (TAPS, 32), 1)
@@ -225,7 +228,8 @@
         jnp.concatenate(gated, axis=1).reshape(NODES, 16, SIDE).astype(jnp.bfloat16)
     )
 
-    jumps = (0, 2, -2)
+    jumps = (2, -2, 1, -1, 0)
+    pl.semaphore_wait(ready, 4)
     b_copies = []
     for group, jump in enumerate(jumps):
         copies = [
@@ -240,17 +244,17 @@
             for i, target in enumerate(targets + ([c] if jump else []))
         ]
         b_copies.append(copies)
-    for group in (1, 2, 0):
-        for copy in b_copies[group]:
+    for copies in b_copies:
+        for copy in copies:
             copy.start()
-        sent += b_copies[group]
-    out_recv[0, c] = out_send[c]
-
-    def hop(owner, part, send_sem, recv_sem, index, target):
-        block = gath.at[owner] if part is None else gath.at[owner, pl.ds(part * 16, 16)]
+        sent += copies
+    out_recv[4, c] = out_send[c]
+
+    def hop(height, half, send_sem, recv_sem, index, target, side=0):
+        rows = pl.ds(0, 32) if half is None else pl.ds(half * 16, 16)
         return pltpu.make_async_remote_copy(
-            src_ref=block,
-            dst_ref=block,
+            src_ref=gath.at[0, height, rows],
+            dst_ref=gath.at[side, height, rows],
             send_sem=send_sem.at[index],
             recv_sem=recv_sem.at[index],
             device_id={"ch": target},
@@ -261,42 +265,36 @@
         copy.start()
         sent.append(copy)
 
-    def share(index, owner, part=None):
-        begin(hop(owner, part, pair_send, pair_recv, index, partner))
+    def share(index, height, half=None):
+        begin(hop(height, half, pair_send, pair_recv, index, partner, 1))
 
     for group, jump in enumerate(jumps):
         for copy in b_copies[group]:
             copy.wait_recv()
-        owner = plane(-jump)
+        height = (z + ROUND - jump) % ROUND
         wide[...] = out_recv[group].astype(jnp.float32).reshape(2 * SIDE, SIDE)
         for row in range(8):
-            gath[owner, :, row * SIDE : (row + 1) * SIDE] = wide[
+            gath[0, height, :, row * SIDE : (row + 1) * SIDE] = wide[
                 pl.ds(row, 32, stride=8), :
             ].astype(jnp.bfloat16)
-        if jump == 0:
-            begin(hop(owner, None, z_send, z_recv, 0, plane(1)))
-            begin(hop(owner, None, z_send, z_recv, 1, plane(-1)))
-        elif jump > 0:
-            begin(hop(owner, 0, z_send, z_recv, 4, plane(2)))
-            begin(hop(owner, None, z_send, z_recv, 2, plane(1)))
-        else:
-            begin(hop(owner, 1, z_send, z_recv, 5, plane(-2)))
-            begin(hop(owner, None, z_send, z_recv, 3, plane(-1)))
-        share(group, owner)
-    for index, jump, part in (
-        (0, -1, None), (1, 1, None), (2, -3, None), (3, 3, None), (4, 4, 0), (5, 4, 1),
-    ):
-        owner = plane(jump)
-        hop(owner, part, z_send, z_recv, index, plane(1)).wait_recv()
-        share(3 + index, owner, part)
-    for index, part in enumerate((None,) * 7 + (0, 1)):
-        hop(h, part, pair_send, pair_recv, index, partner).wait_recv()
+        if jump in (2, -2):
+            begin(hop(height, group, z_send, z_recv, 2 + group, plane(jump)))
+            begin(hop(height, None, z_send, z_recv, group, plane(jump // 2)))
+        share(group, height)
+    for index, jump, half in ((0, -3, None), (1, 3, None), (2, 4, 0), (3, 4, 1)):
+        height = (z + ROUND + jump) % ROUND
+        hop(height, half, z_send, z_recv, index, plane(1)).wait_recv()
+        share(5 + index, height, half)
+    columns = [slice(i * CHUNK, (i + 1) * CHUNK) for i in range(1024 // CHUNK)]
+    for lanes in columns:
+        total[:, lanes] = mm(picked[:, :256], gath[0, :, :, lanes].reshape(256, CHUNK))
+    for index, half in enumerate((None,) * 7 + (0, 1)):
+        hop(z, half, pair_send, pair_recv, index, partner, 1).wait_recv()
+    for lanes in columns:
+        rest = mm(picked[:, 256:], gath[1, :, :, lanes].reshape(256, CHUNK))
+        out[:, lanes] = (total[:, lanes] + rest).astype(jnp.bfloat16)
     for copy in sent:
         copy.wait_send()
-
-
-def project(weight, values, out):
-    out[...] = mm(weight[...], values[...]).astype(jnp.bfloat16)
 
 
 def solution(mesh):
@@ -305,10 +303,12 @@
     peers = NODES - 1
 
     def local(qkv, short_taps, long_filter, skip_gain, out_weight):
-        gathered = pl.pallas_call(
+        operands = [qkv, jnp.swapaxes(short_taps, 1, 2), long_filter, skip_gain, out_weight]
+        operands += [jnp.asarray(t) for t in consts]
+        return pl.pallas_call(
             kernel,
-            out_shape=jax.ShapeDtypeStruct((NODES, 32, 1024), jnp.bfloat16),
-            in_specs=[pl.BlockSpec(memory_space=pl.ANY)] * 9,
+            out_shape=jax.ShapeDtypeStruct((512, 1024), jnp.bfloat16),
+            in_specs=[pl.BlockSpec(memory_space=pltpu.HBM)] * 10,
             out_specs=pl.BlockSpec(memory_space=pltpu.VMEM),
             scratch_shapes=[
                 pltpu.VMEM((3, 32, 1024), jnp.bfloat16),
@@ -320,36 +320,33 @@
                 pltpu.VMEM((2, 256, 256), jnp.bfloat16),
                 pltpu.VMEM((2, 256, 256), jnp.bfloat16),
                 pltpu.VMEM((2, SIDE, 256), jnp.bfloat16),
+                pltpu.VMEM((512, 512), jnp.bfloat16),
+                pltpu.VMEM((512, 512), jnp.bfloat16),
+                pltpu.VMEM((2, ROUND, 32, 1024), jnp.bfloat16),
+                pltpu.VMEM((512, 1024), jnp.float32),
                 pltpu.VMEM((256, SIDE), jnp.float32),
                 pltpu.VMEM((NODES, 4, 16, SIDE), jnp.bfloat16),
                 pltpu.VMEM((NODES, 4, 16, SIDE), jnp.bfloat16),
                 pltpu.VMEM((NODES, 16, SIDE), jnp.bfloat16),
-                pltpu.VMEM((3, NODES, 16, SIDE), jnp.bfloat16),
+                pltpu.VMEM((5, NODES, 16, SIDE), jnp.bfloat16),
                 dma((2,)),
-                dma((7,)),
+                dma((8,)),
                 dma((peers,)),
                 dma((peers,)),
                 dma((peers,)),
                 dma((peers,)),
-                dma((3, NODES)),
-                dma((3, NODES)),
-                dma((6,)),
-                dma((6,)),
+                dma((5, NODES)),
+                dma((5, NODES)),
+                dma((4,)),
+                dma((4,)),
                 dma((9,)),
                 dma((9,)),
+                pltpu.SemaphoreType.REGULAR,
             ],
-            compiler_params=pltpu.CompilerParams(collective_id=0, has_side_effects=True),
-        )(qkv, jnp.swapaxes(short_taps, 1, 2), long_filter, skip_gain, *[jnp.asarray(t) for t in consts])
-        return pl.pallas_call(
-            project,
-            grid=(4,),
-            out_shape=jax.ShapeDtypeStruct((512, 1024), jnp.bfloat16),
-            in_specs=[
-                pl.BlockSpec((512, 512), lambda i: (0, 0)),
-                pl.BlockSpec((512, 256), lambda i: (0, i)),
-            ],
-            out_specs=pl.BlockSpec((512, 256), lambda i: (0, i)),
-        )(out_weight, gathered.reshape(NODES * 32, 1024))
+            compiler_params=pltpu.CompilerParams(
+                collective_id=0, has_side_effects=True, vmem_limit_bytes=GRANT
+            ),
+        )(*[pltpu.with_memory_space_constraint(v, pltpu.HBM) for v in operands])
 
     placed = (P(None, "ch", "ctx"), P(None, "ch", None), P("ch", "ctx"), P("ch"), P("ch", None))
     return jax.shard_map(

time: 37.8 us -> 33.6 us (0.89)
  Pallas kernels: 37.6 us -> 32.5 us
  local copies, waits for them, and re-layouts: 0 us -> 0.97 us
    pallas_call x2 -> x1, Pallas kernels: 37.6 us -> 32.5 us  [local(): pl.pallas_call(kernel, out_shape=jax.ShapeDtypeStruct((512, 1024), jnp.bf...]
    unnamed x0 -> x1, local copies, waits for them, and re-layouts: none -> 0.97 us
where the time goes in v2:
time: 33.6 us; the launch traced here: 33.5 us
  Pallas kernels  32.5 us (97%)
  local copies, waits for them, and re-layouts  0.97 us (3%)
    pallas_call x1, Pallas kernels, local(): pl.pallas_call(kernel, out_shape=jax.ShapeDtypeStruct((512, 1024), jnp.bf...  32.5 us
    unnamed x1, local copies, waits for them, and re-layouts  0.97 us

profile of v2, /device:TPU:1, one launch (start us, length us, event | category | flops | bytes accessed | tf_op | source)
XLA Modules:
  0.0 33.5 jit_solution(16365841856048239154)
XLA Ops:
  0.0 32.5 %shard_map.100 = bf16[512,1024]{1,0:T(8,128)(2,1)S(1)} custom-call(bf16[3,32,1024]{2,1,0:T(8,128)(2,1)} %qkv_in.1, f32[3,7,32]{2,1,0:T(8,128)} %bitcast.1, f32[32,1024]{1,0:T(8,128)} %filt_in.1, f32[32]{0:T(128)} %skip_in.1, bf16[512,512]{1,0:T(8,128)(2,1)} %weight_in.1, bf16[256,256]{1,0:T(8,128)(2,1)} %constant.10.clone.first_in, ...), custom_call_target="tpu_custom_call" | custom-call | tf_op jit(solution)/shard_map/pallas_call | solution.py:308
  32.5 1.0 %copy.12 = bf16[512,1024]{1,0:T(8,128)(2,1)} copy(bf16[512,1024]{1,0:T(8,128)(2,1)S(1)} %shard_map.100) | data formatting | bytes 2097152

commit v3 on v2

--- a/solution.py
+++ b/solution.py
@@ -102,7 +102,8 @@
     for target in targets:
         pl.semaphore_signal(barrier, inc=1, device_id={"ctx": target}, device_id_type=MESH)
     for jump in (1, -1, 2, -2):
-        pl.semaphore_signal(barrier, inc=1, device_id={"ch": plane(jump)}, device_id_type=MESH)
+        for target in (plane(jump), plane(jump) + partner - h):
+            pl.semaphore_signal(barrier, inc=1, device_id={"ch": target}, device_id_type=MESH)
     pl.semaphore_signal(barrier, inc=1, device_id={"ch": partner}, device_id_type=MESH)
     for copy in others:
         copy.start()
@@ -116,7 +117,7 @@
             wide[pl.ds(row, 32, stride=8), :] = block.astype(jnp.float32)
         send[:, stream] = wide[...].reshape(NODES, 16, SIDE).astype(jnp.bfloat16)
 
-    pl.semaphore_wait(barrier, NODES - 1 + 5)
+    pl.semaphore_wait(barrier, NODES - 1 + 9)
     for jump in (1, -1, 2, -2):
         pl.semaphore_signal(ready, inc=1, device_id={"ch": plane(jump)}, device_id_type=MESH)
     a_copies = [
@@ -237,7 +238,7 @@
                 src_ref=out_send.at[target],
                 dst_ref=out_recv.at[group, c],
                 send_sem=b_send.at[group, i],
-                recv_sem=b_recv.at[group, i],
+                recv_sem=b_recv.at[group, c],
                 device_id={"ctx": target, "ch": plane(jump)},
                 device_id_type=MESH,
             )
@@ -250,8 +251,11 @@
         sent += copies
     out_recv[4, c] = out_send[c]
 
+    near = y // 2
+
     def hop(height, half, send_sem, recv_sem, index, target, side=0):
-        rows = pl.ds(0, 32) if half is None else pl.ds(half * 16, 16)
+        first = 0 if half is None else pl.multiple_of((near + half) % 2 * 16, 16)
+        rows = pl.ds(first, 32 if half is None else 16)
         return pltpu.make_async_remote_copy(
             src_ref=gath.at[0, height, rows],
             dst_ref=gath.at[side, height, rows],
@@ -268,28 +272,63 @@
     def share(index, height, half=None):
         begin(hop(height, half, pair_send, pair_recv, index, partner, 1))
 
-    for group, jump in enumerate(jumps):
-        for copy in b_copies[group]:
-            copy.wait_recv()
+    def landed(group, source):
+        pltpu.make_async_remote_copy(
+            src_ref=out_send.at[0],
+            dst_ref=out_recv.at[group, source],
+            send_sem=b_send.at[group, 0],
+            recv_sem=b_recv.at[group, source],
+            device_id={"ctx": targets[0], "ch": h},
+            device_id_type=MESH,
+        ).wait_recv()
+
+    for half in range(2):
+        part = (near + half) % 2
+        for group, jump in ((0, 2), (1, -2)):
+            for member in range(8):
+                landed(group, part * 8 + member)
+            height = (z + ROUND - jump) % ROUND
+            piece = out_recv[group, pl.ds(part * 8, 8)].astype(jnp.float32)
+            rows = wide.at[pl.ds(group * SIDE, SIDE)]
+            rows[...] = piece.reshape(SIDE, SIDE)
+            first = pl.multiple_of(part * 16, 16)
+            for row in range(8):
+                gath[0, height, pl.ds(first, 16), row * SIDE : (row + 1) * SIDE] = rows[
+                    pl.ds(row, 16, stride=8), :
+                ].astype(jnp.bfloat16)
+            for side in range(1 + half):
+                across = side * (partner - h)
+                if half == group:
+                    index = 4 + half + 2 * side
+                    begin(hop(height, half, z_send, z_recv, index, plane(jump) + across, side))
+                index = 2 * half + group if side == 0 else 8 + group
+                begin(hop(height, half, z_send, z_recv, index, plane(jump // 2) + across, side))
+    for group in (2, 3, 4):
+        jump = jumps[group]
+        for source in sources if jump == 0 else sources + [c]:
+            landed(group, source)
         height = (z + ROUND - jump) % ROUND
         wide[...] = out_recv[group].astype(jnp.float32).reshape(2 * SIDE, SIDE)
         for row in range(8):
             gath[0, height, :, row * SIDE : (row + 1) * SIDE] = wide[
                 pl.ds(row, 32, stride=8), :
             ].astype(jnp.bfloat16)
-        if jump in (2, -2):
-            begin(hop(height, group, z_send, z_recv, 2 + group, plane(jump)))
-            begin(hop(height, None, z_send, z_recv, group, plane(jump // 2)))
-        share(group, height)
-    for index, jump, half in ((0, -3, None), (1, 3, None), (2, 4, 0), (3, 4, 1)):
+    for group, jump in enumerate(jumps):
+        share(group, (z + ROUND - jump) % ROUND)
+    arrivals = ((0, -3, 0), (1, 3, 0), (4, 4, 0), (2, -3, 1), (3, 3, 1), (5, 4, 1))
+    for order, (index, jump, half) in enumerate(arrivals):
         height = (z + ROUND + jump) % ROUND
         hop(height, half, z_send, z_recv, index, plane(1)).wait_recv()
-        share(5 + index, height, half)
+        if half == 0:
+            share(5 + order, height, half)
     columns = [slice(i * CHUNK, (i + 1) * CHUNK) for i in range(1024 // CHUNK)]
     for lanes in columns:
         total[:, lanes] = mm(picked[:, :256], gath[0, :, :, lanes].reshape(256, CHUNK))
-    for index, half in enumerate((None,) * 7 + (0, 1)):
+    for index in range(8):
+        half = None if index < 5 else 0
         hop(z, half, pair_send, pair_recv, index, partner, 1).wait_recv()
+    for index in (8, 9, 7):
+        hop(z, 1, z_send, z_recv, index, partner, 1).wait_recv()
     for lanes in columns:
         rest = mm(picked[:, 256:], gath[1, :, :, lanes].reshape(256, CHUNK))
         out[:, lanes] = (total[:, lanes] + rest).astype(jnp.bfloat16)
@@ -337,10 +376,10 @@
                 dma((peers,)),
                 dma((5, NODES)),
                 dma((5, NODES)),
-                dma((4,)),
-                dma((4,)),
-                dma((9,)),
-                dma((9,)),
+                dma((10,)),
+                dma((10,)),
+                dma((8,)),
+                dma((8,)),
                 pltpu.SemaphoreType.REGULAR,
             ],
             compiler_params=pltpu.CompilerParams(

time: 33.6 us -> 32.7 us (0.973)
  Pallas kernels: 32.5 us -> 31.6 us
    pallas_call x1, Pallas kernels: 32.5 us -> 31.6 us  [local(): pl.pallas_call(kernel, out_shape=jax.ShapeDtypeStruct((512, 1024), jnp.bf...]
where the time goes in v3:
time: 32.7 us; the launch traced here: 32.6 us
  Pallas kernels  31.6 us (97%)
  local copies, waits for them, and re-layouts  0.97 us (3%)
    pallas_call x1, Pallas kernels, local(): pl.pallas_call(kernel, out_shape=jax.ShapeDtypeStruct((512, 1024), jnp.bf...  31.6 us
    unnamed x1, local copies, waits for them, and re-layouts  0.97 us

profile of v3, /device:TPU:1, one launch (start us, length us, event | category | flops | bytes accessed | tf_op | source)
XLA Modules:
  0.0 32.6 jit_solution(379566537255597375)
XLA Ops:
  0.0 31.6 %shard_map.100 = bf16[512,1024]{1,0:T(8,128)(2,1)S(1)} custom-call(bf16[3,32,1024]{2,1,0:T(8,128)(2,1)} %qkv_in.1, f32[3,7,32]{2,1,0:T(8,128)} %bitcast.1, f32[32,1024]{1,0:T(8,128)} %filt_in.1, f32[32]{0:T(128)} %skip_in.1, bf16[512,512]{1,0:T(8,128)(2,1)} %weight_in.1, bf16[256,256]{1,0:T(8,128)(2,1)} %constant.10.clone.first_in, ...), custom_call_target="tpu_custom_call" | custom-call | tf_op jit(solution)/shard_map/pallas_call | solution.py:347
  31.6 1.0 %copy.12 = bf16[512,1024]{1,0:T(8,128)(2,1)} copy(bf16[512,1024]{1,0:T(8,128)(2,1)S(1)} %shard_map.100) | data formatting | bytes 2097152

commit v4 on v3

--- a/solution.py
+++ b/solution.py
@@ -65,9 +65,9 @@
 
 def kernel(
     qkv_in, taps_in, filt_in, skip_in, weight_in, first_in, twist_in, fwd_in, inv_in, last_in,
-    out,
+    total, picked_rest, rest,
     qkv, taps, filt, skip, first, twist, fwd, inv, last,
-    weight, picked, gath, total, wide, send, recv, out_send, out_recv,
+    weight, picked, gath, wide, send, recv, out_send, out_recv,
     load_sem, tab_sem, a_send, a_recv, q_send, q_recv, b_send, b_recv,
     z_send, z_recv, pair_send, pair_recv, ready,
 ):
@@ -156,7 +156,9 @@
     wanted = (wanted // 32) % ROUND * 64 + holder * 32 + wanted % 32
     given = lax.broadcasted_iota(jnp.int32, (512, 512), 0)
     chosen = jnp.where(given == wanted, 1.0, 0.0).astype(jnp.bfloat16)
-    picked[...] = mm(weight[...], chosen).astype(jnp.bfloat16)
+    ordered = mm(weight[...], chosen).astype(jnp.bfloat16)
+    picked[...] = ordered[:, :256]
+    picked_rest[...] = ordered[:, 256:]
 
     lane = lax.broadcasted_iota(jnp.int32, (SIDE, SIDE), 1)
     spot = lax.broadcasted_iota(jnp.int32, (TAPS, 32), 1)
@@ -257,8 +259,8 @@
         first = 0 if half is None else pl.multiple_of((near + half) % 2 * 16, 16)
         rows = pl.ds(first, 32 if half is None else 16)
         return pltpu.make_async_remote_copy(
-            src_ref=gath.at[0, height, rows],
-            dst_ref=gath.at[side, height, rows],
+            src_ref=gath.at[height, rows],
+            dst_ref=(gath, rest)[side].at[height, rows],
             send_sem=send_sem.at[index],
             recv_sem=recv_sem.at[index],
             device_id={"ch": target},
@@ -293,7 +295,7 @@
             rows[...] = piece.reshape(SIDE, SIDE)
             first = pl.multiple_of(part * 16, 16)
             for row in range(8):
-                gath[0, height, pl.ds(first, 16), row * SIDE : (row + 1) * SIDE] = rows[
+                gath[height, pl.ds(first, 16), row * SIDE : (row + 1) * SIDE] = rows[
                     pl.ds(row, 16, stride=8), :
                 ].astype(jnp.bfloat16)
             for side in range(1 + half):
@@ -310,7 +312,7 @@
         height = (z + ROUND - jump) % ROUND
         wide[...] = out_recv[group].astype(jnp.float32).reshape(2 * SIDE, SIDE)
         for row in range(8):
-            gath[0, height, :, row * SIDE : (row + 1) * SIDE] = wide[
+            gath[height, :, row * SIDE : (row + 1) * SIDE] = wide[
                 pl.ds(row, 32, stride=8), :
             ].astype(jnp.bfloat16)
     for group, jump in enumerate(jumps):
@@ -323,17 +325,27 @@
             share(5 + order, height, half)
     columns = [slice(i * CHUNK, (i + 1) * CHUNK) for i in range(1024 // CHUNK)]
     for lanes in columns:
-        total[:, lanes] = mm(picked[:, :256], gath[0, :, :, lanes].reshape(256, CHUNK))
+        total[:, lanes] = mm(picked[...], gath[:, :, lanes].reshape(256, CHUNK))
     for index in range(8):
         half = None if index < 5 else 0
         hop(z, half, pair_send, pair_recv, index, partner, 1).wait_recv()
     for index in (8, 9, 7):
         hop(z, 1, z_send, z_recv, index, partner, 1).wait_recv()
-    for lanes in columns:
-        rest = mm(picked[:, 256:], gath[1, :, :, lanes].reshape(256, CHUNK))
-        out[:, lanes] = (total[:, lanes] + rest).astype(jnp.bfloat16)
     for copy in sent:
         copy.wait_send()
+
+
+def finish(total, picked, values, out, stage, sem):
+    copies = []
+    for i in range(1024 // CHUNK):
+        rows = pl.ds(i * (512 * CHUNK // 1024), 512 * CHUNK // 1024)
+        late = mm(picked[rows, :], values[...])
+        stage[rows, :] = (total[rows, :] + late).astype(jnp.bfloat16)
+        copy = pltpu.make_async_copy(stage.at[rows], out.at[rows], sem.at[i])
+        copy.start()
+        copies.append(copy)
+    for copy in copies:
+        copy.wait()
 
 
 def solution(mesh):
@@ -344,11 +356,15 @@
     def local(qkv, short_taps, long_filter, skip_gain, out_weight):
         operands = [qkv, jnp.swapaxes(short_taps, 1, 2), long_filter, skip_gain, out_weight]
         operands += [jnp.asarray(t) for t in consts]
-        return pl.pallas_call(
+        total, picked, rest = pl.pallas_call(
             kernel,
-            out_shape=jax.ShapeDtypeStruct((512, 1024), jnp.bfloat16),
+            out_shape=(
+                jax.ShapeDtypeStruct((512, 1024), jnp.float32),
+                jax.ShapeDtypeStruct((512, 256), jnp.bfloat16),
+                jax.ShapeDtypeStruct((ROUND, 32, 1024), jnp.bfloat16),
+            ),
             in_specs=[pl.BlockSpec(memory_space=pltpu.HBM)] * 10,
-            out_specs=pl.BlockSpec(memory_space=pltpu.VMEM),
+            out_specs=[pl.BlockSpec(memory_space=pltpu.VMEM)] * 3,
             scratch_shapes=[
                 pltpu.VMEM((3, 32, 1024), jnp.bfloat16),
                 pltpu.VMEM((3, TAPS, 32), jnp.float32),
@@ -360,9 +376,8 @@
                 pltpu.VMEM((2, 256, 256), jnp.bfloat16),
                 pltpu.VMEM((2, SIDE, 256), jnp.bfloat16),
                 pltpu.VMEM((512, 512), jnp.bfloat16),
-                pltpu.VMEM((512, 512), jnp.bfloat16),
-                pltpu.VMEM((2, ROUND, 32, 1024), jnp.bfloat16),
-                pltpu.VMEM((512, 1024), jnp.float32),
+                pltpu.VMEM((512, 256), jnp.bfloat16),
+                pltpu.VMEM((ROUND, 32, 1024), jnp.bfloat16),
                 pltpu.VMEM((256, SIDE), jnp.float32),
                 pltpu.VMEM((NODES, 4, 16, SIDE), jnp.bfloat16),
                 pltpu.VMEM((NODES, 4, 16, SIDE), jnp.bfloat16),
@@ -386,6 +401,14 @@
                 collective_id=0, has_side_effects=True, vmem_limit_bytes=GRANT
             ),
         )(*[pltpu.with_memory_space_constraint(v, pltpu.HBM) for v in operands])
+        return pl.pallas_call(
+            finish,
+            out_shape=jax.ShapeDtypeStruct((512, 1024), jnp.bfloat16),
+            in_specs=[pl.BlockSpec(memory_space=pltpu.VMEM)] * 3,
+            out_specs=pl.BlockSpec(memory_space=pl.ANY),
+            scratch_shapes=[pltpu.VMEM((512, 1024), jnp.bfloat16), dma((1024 // CHUNK,))],
+            compiler_params=pltpu.CompilerParams(vmem_limit_bytes=GRANT),
+        )(total, picked, rest.reshape(256, 1024))
 
     placed = (P(None, "ch", "ctx"), P(None, "ch", None), P("ch", "ctx"), P("ch"), P("ch", None))
     return jax.shard_map(

time: 32.7 us -> 32.5 us (level)
  local copies, waits for them, and re-layouts: 0.97 us -> 0 us
  Pallas kernels: 31.6 us -> 32.4 us
    unnamed x1 -> x0, local copies, waits for them, and re-layouts: 0.97 us -> none
    pallas_call x1 -> x2, Pallas kernels: 31.6 us -> 32.4 us  [the longest x1 31.2 us: local(): pl.pallas_call(kernel, out_shape=(jax.ShapeDtypeStruct((512, 1024), jnp.f...]
where the time goes in v4:
time: 32.5 us; the launch traced here: 32.4 us
  Pallas kernels  32.4 us (100%)
    pallas_call x1, Pallas kernels, local(): pl.pallas_call(kernel, out_shape=(jax.ShapeDtypeStruct((512, 1024), jnp.f...  31.2 us
    pallas_call x1, Pallas kernels, local(): pl.pallas_call(finish, out_shape=jax.ShapeDtypeStruct((512, 1024), jnp.bf...  1.24 us

profile of v4, /device:TPU:1, one launch (start us, length us, event | category | flops | bytes accessed | tf_op | source)
XLA Modules:
  0.0 32.4 jit_solution(15415069175111358449)
XLA Ops:
  0.0 31.2 %shard_map.100 = (f32[512,1024]{1,0:T(8,128)S(1)}, bf16[512,256]{1,0:T(8,128)(2,1)S(1)}, bf16[8,32,1024]{2,1,0:T(8,128)(2,1)S(1)}) custom-call(bf16[3,32,1024]{2,1,0:T(8,128)(2,1)} %qkv_in.1, f32[3,7,32]{2,1,0:T(8,128)} %bitcast.3, f32[32,1024]{1,0:T(8,128)} %filt_in.1, f32[32]{0:T(128)} %skip_in.1, bf16[512,512]{1,0:T(8,128)(2,1)} %weight_in.1, ...), custom_call_target="tpu_custom_call" | custom-call | tf_op jit(solution)/shard_map/pallas_call | solution.py:359
  31.2 1.2 %shard_map.101 = bf16[512,1024]{1,0:T(8,128)(2,1)} custom-call(f32[512,1024]{1,0:T(8,128)S(1)} %get-tuple-element.8.total, bf16[512,256]{1,0:T(8,128)(2,1)S(1)} %get-tuple-element.9.picked, bf16[256,1024]{1,0:T(8,128)(2,1)S(1)} %bitcast.2), custom_call_target="tpu_custom_call" | custom-call | tf_op jit(solution)/shard_map/pallas_call | solution.py:404

commit v5 on v3

--- a/solution.py
+++ b/solution.py
@@ -200,6 +200,10 @@
     k_rows, v_rows = stream_of(1), stream_of(2)
     product = [short(k_rows[n], 1, n) * short(v_rows[n], 2, n) for n in range(2)]
     spec_p = spectrum([p.astype(jnp.bfloat16) for p in product])
+    for copy in q_copies:
+        copy.wait_recv()
+    q_rows = stream_of(0)
+    queries = [short(q_rows[n], 0, n) for n in range(2)]
     p_re, p_im = spec_p[:, :SIDE], spec_p[:, SIDE:]
     f_re, f_im = spec_f[:, :SIDE], spec_f[:, SIDE:]
     joined = jnp.concatenate([p_re * f_re - p_im * f_im, p_re * f_im + p_im * f_re], axis=1)
@@ -217,14 +221,10 @@
     high, low = parts(jnp.concatenate(columns, axis=1))
     convolved = mm(last[0], high) + mm(last[1], high) + mm(last[0], low)
 
-    for copy in q_copies:
-        copy.wait_recv()
-    q_rows = stream_of(0)
     gated = []
     for n in range(2):
-        query = short(q_rows[n], 0, n)
         mixed = convolved[:, n * SIDE : (n + 1) * SIDE] + skip[2 * c + n] * product[n]
-        gated.append((query * mixed).reshape(NODES, 1, 8, SIDE))
+        gated.append((queries[n] * mixed).reshape(NODES, 1, 8, SIDE))
     out_send[...] = (
         jnp.concatenate(gated, axis=1).reshape(NODES, 16, SIDE).astype(jnp.bfloat16)
     )

time: 32.7 us -> 32.6 us (level)
  no operation moved by 1% of the time
where the time goes in v5:
time: 32.6 us; the launch traced here: 32.5 us
  Pallas kernels  31.5 us (97%)
  local copies, waits for them, and re-layouts  0.97 us (3%)
    pallas_call x1, Pallas kernels, local(): pl.pallas_call(kernel, out_shape=jax.ShapeDtypeStruct((512, 1024), jnp.bf...  31.5 us
    unnamed x1, local copies, waits for them, and re-layouts  0.97 us

profile of v5, /device:TPU:1, one launch (start us, length us, event | category | flops | bytes accessed | tf_op | source)
XLA Modules:
  0.0 32.5 jit_solution(7842030215089735228)
XLA Ops:
  0.0 31.5 %shard_map.100 = bf16[512,1024]{1,0:T(8,128)(2,1)S(1)} custom-call(bf16[3,32,1024]{2,1,0:T(8,128)(2,1)} %qkv_in.1, f32[3,7,32]{2,1,0:T(8,128)} %bitcast.1, f32[32,1024]{1,0:T(8,128)} %filt_in.1, f32[32]{0:T(128)} %skip_in.1, bf16[512,512]{1,0:T(8,128)(2,1)} %weight_in.1, bf16[256,256]{1,0:T(8,128)(2,1)} %constant.10.clone.first_in, ...), custom_call_target="tpu_custom_call" | custom-call | tf_op jit(solution)/shard_map/pallas_call | solution.py:347
  31.5 1.0 %copy.12 = bf16[512,1024]{1,0:T(8,128)(2,1)} copy(bf16[512,1024]{1,0:T(8,128)(2,1)S(1)} %shard_map.100) | data formatting | bytes 2097152
